TPU v7x, 32 devices: a whole 2x2x4 slice. The times are simulated.
32 devices in a mesh: groups: 2 (over y), space: 4 (over z), wave: 4 (over x, core).
Axes of the slice: x: 2, y: 2, z: 4, core: 2. Of those that a mesh axis runs over, the one named last changes fastest.
Arguments:
- density: float32 [512, 16, 128], P(('groups', 'space')), parts along dimension 0, may hold values from -6 to 6
- even_taps: float32 [15], replicated, may hold values from -1.5 to 1.5
- odd_taps: float32 [15], replicated, may hold values from -1.5 to 1.5
- low_taps: float32 [15], replicated, may hold values from -1.5 to 1.5
- wavelets: int32 [40, 2], replicated, may hold values from 0 to 2, as said below
- pairs: int32 [32, 2], replicated, may hold values from -1 to 39, as said below
Outputs:
- second: float32 [32, 256, 8, 64], P('wave', ('groups', 'space')), parts along dimension 1
There are 2 independent parts, one for each index of `groups`. A program takes and returns all parts, laid end to end along the dimension named above; an argument that names none is the same for every part. Nothing has to cross between parts.
Inputs may be any that keep to these rules, and one draw needn't show every extreme that they name: `wavelets`: column 0 is a dilation level below 3, column 1 an orientation 0, 1 or 2. Rows below 5 have levels below 2; the last row has level 2. `pairs`: the slots form aligned blocks of 8 rows, one block for each index of wave. In every block the live rows come first and at least one is live; some block has all 8 rows live. A live row holds a first-order field below 5 and a wavelet row of 5 or more whose level is above that field's level; a dead row is (-1, 0).
All inputs are finite; a program needn't handle non-finite values.
Results may differ from a plain program's by a relative error of at most 0.0003.
Values sent between devices are 32-bit elements; how exact they have to be, the bound alone decides.
A program may use at most 64 MiB of HBM per device.

v0:
```python
import functools

import jax
import jax.numpy as jnp
from jax import lax
from jax.experimental import pallas as pl
from jax.experimental.pallas import tpu as pltpu
from jax.sharding import PartitionSpec as P

NFIRST = 5
REACH1 = 14
REACH2 = 28
HALO = REACH1 + REACH2
GROUP = 8
BF = jnp.bfloat16


def split_outside(t):
    hi = lax.reduce_precision(t, 8, 7)
    return hi.astype(BF), (t - hi).astype(BF)


def band(diff, taps, dilation):
    count = taps.shape[0]
    total = jnp.zeros(diff.shape, jnp.float32)
    for t in range(count):
        total = jnp.where(diff == (t - count // 2) * dilation, taps[t], total)
    return total


def tables(filters, ny, nz):
    def zdiff(n_out, stride):
        i = lax.broadcasted_iota(jnp.int32, (nz, n_out), 0)
        j = lax.broadcasted_iota(jnp.int32, (nz, n_out), 1)
        return i - j * stride

    def ytable(taps, d, stride):
        n_out = ny // stride
        r = lax.broadcasted_iota(jnp.int32, (GROUP * n_out, GROUP * ny), 0)
        c = lax.broadcasted_iota(jnp.int32, (GROUP * n_out, GROUP * ny), 1)
        t = band(c % ny - (r % n_out) * stride, taps, d)
        hi, lo = split_outside(jnp.where(r // n_out == c // ny, t, 0.0))
        return jnp.concatenate([hi, hi, lo], axis=1)

    z1, y1, z2, y2 = [], [], [], []
    for level in (0, 1):
        for taps in filters:
            hi, lo = split_outside(band(zdiff(nz, 1), taps, 1 << level))
            z1.append(
                jnp.concatenate(
                    [
                        jnp.concatenate([hi, lo], axis=1),
                        jnp.concatenate([hi, jnp.zeros_like(lo)], axis=1),
                    ],
                    axis=0,
                )
            )
            y1.append(ytable(taps, 1 << level, 1))
    for level in (1, 2):
        parts = [split_outside(band(zdiff(nz // 2, 2), taps, 1 << level)) for taps in filters]
        zero = jnp.zeros((nz, nz // 2), BF)
        none = (zero, zero)
        for left, right in ((parts[2], none), (none, parts[2]), (parts[0], parts[1])):
            z2.append(
                jnp.concatenate(
                    [
                        jnp.concatenate([left[0], right[0], left[1], right[1]], axis=1),
                        jnp.concatenate([left[0], right[0], zero, zero], axis=1),
                    ],
                    axis=0,
                )
            )
        for taps in filters:
            y2.append(ytable(taps, 1 << level, 2))
    return jnp.stack(z1), jnp.stack(y1), jnp.stack(z2), jnp.stack(y2)


def halves(v):
    hi = v.astype(BF)
    return hi, (v - hi.astype(jnp.float32)).astype(BF)


def stacked(v):
    hi, lo = halves(v)
    return jnp.concatenate([hi, lo, hi], axis=0)


def beside(v):
    hi, lo = halves(v)
    return jnp.concatenate([hi, lo], axis=1)


def dot(a, b):
    return jnp.dot(a, b, preferred_element_type=jnp.float32)


def folded(r):
    n = r.shape[1] // 2
    return r[:, :n] + r[:, n:]


def xpass(load, tap_sets):
    count = tap_sets[0].shape[0]
    accs = [[None] * GROUP for _ in tap_sets]
    for t in range(count):
        weights = [s[t] for s in tap_sets]
        for k in range(GROUP):
            plane = load(t, k)
            for n, w in enumerate(weights):
                term = w * plane
                accs[n][k] = term if t == 0 else accs[n][k] + term
    return [jnp.concatenate(a, axis=0) for a in accs]


def kernel(
    rows,
    wav,
    pairs,
    even,
    odd,
    low,
    before,
    centre,
    after,
    z1,
    y1,
    z2,
    y2,
    out,
    ext,
    firsts,
    sems,
):
    ny, nz = ext.shape[1], ext.shape[2]
    per_dev = out.shape[0]
    taps_half = even.shape[0] // 2
    fields = rows + 2 * REACH2
    copies = [
        pltpu.make_async_copy(before, ext.at[pl.ds(0, HALO)], sems.at[0]),
        pltpu.make_async_copy(centre, ext.at[pl.ds(HALO, rows)], sems.at[1]),
        pltpu.make_async_copy(after, ext.at[pl.ds(HALO + rows, HALO)], sems.at[2]),
    ]
    for copy in copies:
        copy.start()
    for copy in copies:
        copy.wait()
    space = lax.axis_index("space")
    start = lax.axis_index("wave") * per_dev

    def first_steps(f, orient, unroll):
        level = wav[f, 0]
        d = jnp.left_shift(jnp.int32(1), level)
        tab = level * 3

        def step(i, carry):
            chains = []
            for u in range(unroll):
                base = (i * unroll + u) * GROUP + REACH1

                def load(t, k):
                    return ext[base + k + (t - taps_half) * d]

                xs = xpass(load, (even, odd) if orient == 0 else (low,))
                if orient == 1:
                    src = stacked(xs[0])
                    ys = [dot(y1[tab], src), dot(y1[tab + 1], src)]
                else:
                    ys = [dot(y1[tab + 2], stacked(x)) for x in xs]
                chains.append(ys)
            cols = [beside(jnp.concatenate(c, axis=0)) for c in zip(*chains)]
            if orient == 2:
                re = folded(dot(cols[0], z1[tab]))
                im = folded(dot(cols[0], z1[tab + 1]))
            else:
                re = folded(dot(cols[0], z1[tab + 2]))
                im = folded(dot(cols[1], z1[tab + 2]))
            mag = jnp.sqrt(re * re + im * im + 1e-06)
            planes = unroll * GROUP
            firsts[f, pl.ds(i * planes, planes)] = mag.reshape(planes, ny, nz)
            return carry

        lax.fori_loop(0, fields // (unroll * GROUP), step, 0)

    def do_first(f, carry):
        need = jnp.int32(0)
        for p in range(per_dev):
            need = need + (pairs[start + p, 0] == f).astype(jnp.int32)
        for orient in range(3):

            @pl.when((need > 0) & (wav[f, 1] == orient))
            def _():
                first_steps(f, orient, 3 if fields % (3 * GROUP) == 0 else 1)

        @pl.when(space == 0)
        def _():
            firsts[f, pl.ds(0, REACH2)] = jnp.zeros((REACH2, ny, nz), jnp.float32)

        @pl.when(space == lax.axis_size("space") - 1)
        def _():
            firsts[f, pl.ds(REACH2 + rows, REACH2)] = jnp.zeros((REACH2, ny, nz), jnp.float32)

        return carry

    lax.fori_loop(0, NFIRST, do_first, 0)

    def second_steps(p, f, w, orient):
        level = wav[w, 0]
        d = jnp.left_shift(jnp.int32(1), level)
        tab = (level - 1) * 3
        chains = []
        for g in range(rows // 2 // GROUP):

            def load(t, k):
                return firsts[f, REACH2 + 2 * (g * GROUP + k) + (t - taps_half) * d]

            xs = xpass(load, (even, odd) if orient == 0 else (low,))
            if orient == 1:
                src = stacked(xs[0])
                ys = [dot(y2[tab], src), dot(y2[tab + 1], src)]
            else:
                ys = [dot(y2[tab + 2], stacked(x)) for x in xs]
            chains.append(ys)
        cols = [beside(jnp.concatenate(c, axis=0)) for c in zip(*chains)]
        if orient == 2:
            r = dot(cols[0], z2[tab + 2])
        else:
            r = dot(cols[0], z2[tab]) + dot(cols[1], z2[tab + 1])
        v = folded(r)
        sq = v * v
        total = sq + pltpu.roll(sq, nz // 2, 1)
        mag = jnp.sqrt(total + 1e-06)[:, : nz // 2]
        out[p] = mag.reshape(out.shape[1:])

    def do_pair(p, carry):
        f = pairs[start + p, 0]
        w = pairs[start + p, 1]
        for orient in range(3):

            @pl.when((f >= 0) & (wav[w, 1] == orient))
            def _():
                second_steps(p, f, w, orient)

        @pl.when(f < 0)
        def _():
            out[p] = jnp.zeros(out.shape[1:], jnp.float32)

        return carry

    lax.fori_loop(0, per_dev, do_pair, 0)


def shards(density, even_taps, odd_taps, low_taps, wavelets, pairs):
    rows, ny, nz = density.shape
    count = lax.axis_size("space")
    up = [(i, i + 1) for i in range(count - 1)]
    down = [(j, i) for i, j in up]
    before = lax.ppermute(density[rows - HALO :], "space", up)
    after = lax.ppermute(density[:HALO], "space", down)
    z1, y1, z2, y2 = tables((even_taps, odd_taps, low_taps), ny, nz)
    per_dev = pairs.shape[0] // lax.axis_size("wave")
    smem = pl.BlockSpec(memory_space=pltpu.SMEM)
    vmem = pl.BlockSpec(memory_space=pltpu.VMEM)
    anyw = pl.BlockSpec(memory_space=pl.ANY)
    return pl.pallas_call(
        functools.partial(kernel, rows),
        out_shape=jax.ShapeDtypeStruct((per_dev, rows // 2, ny // 2, nz // 2), jnp.float32),
        in_specs=[smem] * 5 + [anyw] * 3 + [vmem] * 4,
        out_specs=vmem,
        scratch_shapes=[
            pltpu.VMEM((rows + 2 * HALO, ny, nz), jnp.float32),
            pltpu.VMEM((NFIRST, rows + 2 * REACH2, ny, nz), jnp.float32),
            pltpu.SemaphoreType.DMA((3,)),
        ],
        name="scatter",
    )(wavelets, pairs, even_taps, odd_taps, low_taps, before, density, after, z1, y1, z2, y2)


def solution(mesh):
    placed = (P(("groups", "space"), None, None), P(), P(), P(), P(), P())
    return jax.shard_map(
        shards,
        mesh=mesh,
        in_specs=placed,
        out_specs=P("wave", ("groups", "space"), None, None),
        check_vma=False,
    )
```

profile of v0, /device:TPU:0, one launch (start us, length us, event | category | flops | bytes accessed | tf_op | source)
XLA Modules:
  0.0 382.5 jit_solution(6615453371232910828)
XLA Ops:
  0.0 1.2 fusion.170
  1.2 5.0 %collective-permute-start = (f32[42,16,128]{2,1,0:T(8,128)S(1)}, f32[42,16,128]{2,1,0:T(8,128)S(1)}, u32[]{:S(2)}, u32[]{:S(2)}) collective-permute-start(f32[42,16,128]{2,1,0:T(8,128)S(1)} %get-tuple-element.6), channel_id=1, source_target_pairs={{0,4},{4,8},{8,12},{1,5},{5,9},{9,13},{2,6},{6,10},{10,14},{3,7},{... | collective-permute-start | bytes 1032200 | tf_op jit(solution)/shard_map/ppermute | solution.py:257
  6.2 1.3 collective-permute-start.1
  8.3 10.0 %reduce-precision_convert_fusion.14 = (bf16[128,128]{1,0:T(8,128)(2,1)}, bf16[128,128]{1,0:T(8,128)(2,1)S(1)}) fusion(f32[]{:T(128)} %bitcast.14, f32[]{:T(128)} %bitcast.13, f32[]{:T(128)} %bitcast.12, f32[]{:T(128)} %bitcast.11, f32[]{:T(128)} %bitcast.10, f32[]{:T(128)} %bitcast.9, f32[]{:T(128)} %bitcast.8, f32[]{:T(128)} %bitcast.7, f32[]{:T(128)} %bitcast.6, ...), kind=kLoop, calls=%fused_computation.104 | loop fusion | flops 950272 | bytes 65596 | tf_op jit(solution)/shard_map/convert_element_type | solution.py:20
  18.3 10.0 %fusion.54 = (bf16[128,128]{1,0:T(8,128)(2,1)S(1)}, bf16[128,128]{1,0:T(8,128)(2,1)}) fusion(f32[]{:T(128)} %bitcast.14, f32[]{:T(128)} %bitcast.13, f32[]{:T(128)} %bitcast.12, f32[]{:T(128)} %bitcast.11, f32[]{:T(128)} %bitcast.10, f32[]{:T(128)} %bitcast.9, f32[]{:T(128)} %bitcast.8, f32[]{:T(128)} %bitcast.7, f32[]{:T(128)} %bitcast.6, f32[]{:T(128)} %bitcast.5, ...), kind=kLoop, calls=%fused_computation.111 | loop fusion | flops 983040 | bytes 65596 | tf_op jit(solution)/shard_map/convert_element_type | solution.py:20
  28.3 10.0 %fusion.70 = (bf16[128,64]{1,0:T(8,128)(2,1)S(1)}, bf16[128,64]{1,0:T(8,128)(2,1)S(1)}, bf16[128,64]{1,0:T(8,128)(2,1)}, bf16[128,64]{1,0:T(8,128)(2,1)S(1)}) fusion(f32[]{:T(128)} %bitcast.14, f32[]{:T(128)} %bitcast.13, f32[]{:T(128)} %bitcast.12, f32[]{:T(128)} %bitcast.11, f32[]{:T(128)} %bitcast.10, f32[]{:T(128)} %bitcast.9, f32[]{:T(128)} %bitcast.8, ...), kind=kLoop, calls=%fused_computation.127 | loop fusion | flops 507904 | bytes 65852 | tf_op jit(solution)/shard_map/convert_element_type | solution.py:20
  39.1 10.2 %fusion.71 = (bf16[128,64]{1,0:T(8,128)(2,1)}, bf16[128,64]{1,0:T(8,128)(2,1)S(1)}, bf16[128,64]{1,0:T(8,128)(2,1)}, bf16[128,64]{1,0:T(8,128)(2,1)S(1)}) fusion(f32[]{:T(128)} %bitcast.30, f32[]{:T(128)} %bitcast.29, f32[]{:T(128)} %bitcast.28, f32[]{:T(128)} %bitcast.27, f32[]{:T(128)} %bitcast.26, f32[]{:T(128)} %bitcast.25, f32[]{:T(128)} %bitcast.24, ...), kind=kLoop, calls=%fused_computation.128 | loop fusion | flops 507904 | bytes 65852 | tf_op jit(solution)/shard_map/convert_element_type | solution.py:20
  49.2 10.2 %reduce-precision_convert_fusion.13 = (bf16[128,128]{1,0:T(8,128)(2,1)}, bf16[128,128]{1,0:T(8,128)(2,1)}) fusion(f32[]{:T(128)} %bitcast.30, f32[]{:T(128)} %bitcast.29, f32[]{:T(128)} %bitcast.28, f32[]{:T(128)} %bitcast.27, f32[]{:T(128)} %bitcast.26, f32[]{:T(128)} %bitcast.25, f32[]{:T(128)} %bitcast.24, f32[]{:T(128)} %bitcast.23, f32[]{:T(128)} %bitcast.22, ...), kind=kLoop, calls=%fused_computation.102 | loop fusion | flops 950272 | bytes 65596 | tf_op jit(solution)/shard_map/convert_element_type | solution.py:20
  59.4 10.2 %fusion.55 = (bf16[128,128]{1,0:T(8,128)(2,1)}, bf16[128,128]{1,0:T(8,128)(2,1)}) fusion(f32[]{:T(128)} %bitcast.30, f32[]{:T(128)} %bitcast.29, f32[]{:T(128)} %bitcast.28, f32[]{:T(128)} %bitcast.27, f32[]{:T(128)} %bitcast.26, f32[]{:T(128)} %bitcast.25, f32[]{:T(128)} %bitcast.24, f32[]{:T(128)} %bitcast.23, f32[]{:T(128)} %bitcast.22, f32[]{:T(128)} %bitcast.21, ...), kind=kLoop, calls=%fused_computation.112 | loop fusion | flops 983040 | bytes 65596 | tf_op jit(solution)/shard_map/convert_element_type | solution.py:20
  70.3 9.5 %fusion.69 = (bf16[128,64]{1,0:T(8,128)(2,1)S(1)}, bf16[128,64]{1,0:T(8,128)(2,1)S(1)}, bf16[128,64]{1,0:T(8,128)(2,1)S(1)}, bf16[128,64]{1,0:T(8,128)(2,1)S(1)}) fusion(f32[]{:T(128)} %bitcast.46, f32[]{:T(128)} %bitcast.45, f32[]{:T(128)} %bitcast.44, f32[]{:T(128)} %bitcast.43, f32[]{:T(128)} %bitcast.42, f32[]{:T(128)} %bitcast.41, f32[]{:T(128)} %bitcast.40, ...), kind=kLoop, calls=%fused_computation.126 | loop fusion | flops 507904 | bytes 65852 | tf_op jit(solution)/shard_map/convert_element_type | solution.py:20
  79.8 10.0 %reduce-precision_convert_fusion.15 = (bf16[128,128]{1,0:T(8,128)(2,1)}, bf16[128,128]{1,0:T(8,128)(2,1)}) fusion(f32[]{:T(128)} %bitcast.46, f32[]{:T(128)} %bitcast.45, f32[]{:T(128)} %bitcast.44, f32[]{:T(128)} %bitcast.43, f32[]{:T(128)} %bitcast.42, f32[]{:T(128)} %bitcast.41, f32[]{:T(128)} %bitcast.40, f32[]{:T(128)} %bitcast.39, f32[]{:T(128)} %bitcast.38, ...), kind=kLoop, calls=%fused_computation.106 | loop fusion | flops 573440 | bytes 65596 | tf_op jit(solution)/shard_map/convert_element_type | solution.py:20
  89.8 10.0 %reduce-precision_convert_fusion.12 = (bf16[128,128]{1,0:T(8,128)(2,1)}, bf16[128,128]{1,0:T(8,128)(2,1)}) fusion(f32[]{:T(128)} %bitcast.46, f32[]{:T(128)} %bitcast.45, f32[]{:T(128)} %bitcast.44, f32[]{:T(128)} %bitcast.43, f32[]{:T(128)} %bitcast.42, f32[]{:T(128)} %bitcast.41, f32[]{:T(128)} %bitcast.40, f32[]{:T(128)} %bitcast.39, f32[]{:T(128)} %bitcast.38, ...), kind=kLoop, calls=%fused_computation.100 | loop fusion | flops 573440 | bytes 65596 | tf_op jit(solution)/shard_map/convert_element_type | solution.py:20
  99.8 9.5 %fusion.60 = bf16[128,128]{1,0:T(8,128)(2,1)S(1)} fusion(f32[]{:T(128)} %bitcast.14, f32[]{:T(128)} %bitcast.13, f32[]{:T(128)} %bitcast.12, f32[]{:T(128)} %bitcast.11, f32[]{:T(128)} %bitcast.10, f32[]{:T(128)} %bitcast.9, f32[]{:T(128)} %bitcast.8, f32[]{:T(128)} %bitcast.7, f32[]{:T(128)} %bitcast.6, f32[]{:T(128)} %bitcast.5, f32[]{:T(128)} %bitcast.4, ...), kind=kLoop, calls=%fused_computation.117 | loop fusion | flops 655360 | bytes 35132 | tf_op jit(solution)/shard_map/convert_element_type | solution.py:20
  109.3 9.5 %reduce-precision_convert_fusion.11 = bf16[128,128]{1,0:T(8,128)(2,1)S(1)} fusion(f32[]{:T(128)} %bitcast.14, f32[]{:T(128)} %bitcast.13, f32[]{:T(128)} %bitcast.12, f32[]{:T(128)} %bitcast.11, f32[]{:T(128)} %bitcast.10, f32[]{:T(128)} %bitcast.9, f32[]{:T(128)} %bitcast.8, f32[]{:T(128)} %bitcast.7, f32[]{:T(128)} %bitcast.6, f32[]{:T(128)} %bitcast.5, ...), kind=kLoop, calls=%fused_computation.98 | loop fusion | flops 638976 | bytes 35132 | tf_op jit(solution)/shard_map/convert_element_type | solution.py:20
  118.8 10.2 %fusion.61 = bf16[128,128]{1,0:T(8,128)(2,1)} fusion(f32[]{:T(128)} %bitcast.30, f32[]{:T(128)} %bitcast.29, f32[]{:T(128)} %bitcast.28, f32[]{:T(128)} %bitcast.27, f32[]{:T(128)} %bitcast.26, f32[]{:T(128)} %bitcast.25, f32[]{:T(128)} %bitcast.24, f32[]{:T(128)} %bitcast.23, f32[]{:T(128)} %bitcast.22, f32[]{:T(128)} %bitcast.21, f32[]{:T(128)} %bitcast.20, ...), kind=kLoop, calls=%fused_computation.118 | loop fusion | flops 655360 | bytes 35132 | tf_op jit(solution)/shard_map/convert_element_type | solution.py:20
  128.9 10.2 %reduce-precision_convert_fusion.10 = bf16[128,128]{1,0:T(8,128)(2,1)} fusion(f32[]{:T(128)} %bitcast.30, f32[]{:T(128)} %bitcast.29, f32[]{:T(128)} %bitcast.28, f32[]{:T(128)} %bitcast.27, f32[]{:T(128)} %bitcast.26, f32[]{:T(128)} %bitcast.25, f32[]{:T(128)} %bitcast.24, f32[]{:T(128)} %bitcast.23, f32[]{:T(128)} %bitcast.22, f32[]{:T(128)} %bitcast.21, ...), kind=kLoop, calls=%fused_computation.96 | loop fusion | flops 638976 | bytes 35132 | tf_op jit(solution)/shard_map/convert_element_type | solution.py:20
  139.2 10.1 %fusion.62 = bf16[128,128]{1,0:T(8,128)(2,1)} fusion(f32[]{:T(128)} %bitcast.46, f32[]{:T(128)} %bitcast.45, f32[]{:T(128)} %bitcast.44, f32[]{:T(128)} %bitcast.43, f32[]{:T(128)} %bitcast.42, f32[]{:T(128)} %bitcast.41, f32[]{:T(128)} %bitcast.40, f32[]{:T(128)} %bitcast.39, f32[]{:T(128)} %bitcast.38, f32[]{:T(128)} %bitcast.37, f32[]{:T(128)} %bitcast.36, ...), kind=kLoop, calls=%fused_computation.119 | loop fusion | flops 655360 | bytes 35132 | tf_op jit(solution)/shard_map/convert_element_type | solution.py:20
  149.2 10.1 %reduce-precision_convert_fusion.9 = bf16[128,128]{1,0:T(8,128)(2,1)} fusion(f32[]{:T(128)} %bitcast.46, f32[]{:T(128)} %bitcast.45, f32[]{:T(128)} %bitcast.44, f32[]{:T(128)} %bitcast.43, f32[]{:T(128)} %bitcast.42, f32[]{:T(128)} %bitcast.41, f32[]{:T(128)} %bitcast.40, f32[]{:T(128)} %bitcast.39, f32[]{:T(128)} %bitcast.38, f32[]{:T(128)} %bitcast.37, ...), kind=kLoop, calls=%fused_computation.94 | loop fusion | flops 638976 | bytes 35132 | tf_op jit(solution)/shard_map/convert_element_type | solution.py:20
  159.3 10.1 %fusion.63 = bf16[128,128]{1,0:T(8,128)(2,1)} fusion(f32[]{:T(128)} %bitcast.14, f32[]{:T(128)} %bitcast.13, f32[]{:T(128)} %bitcast.12, f32[]{:T(128)} %bitcast.11, f32[]{:T(128)} %bitcast.10, f32[]{:T(128)} %bitcast.9, f32[]{:T(128)} %bitcast.8, f32[]{:T(128)} %bitcast.7, f32[]{:T(128)} %bitcast.6, f32[]{:T(128)} %bitcast.5, f32[]{:T(128)} %bitcast.4, ...), kind=kLoop, calls=%fused_computation.120 | loop fusion | flops 655360 | bytes 35132 | tf_op jit(solution)/shard_map/convert_element_type | solution.py:20
  169.4 10.1 %reduce-precision_convert_fusion.8 = bf16[128,128]{1,0:T(8,128)(2,1)} fusion(f32[]{:T(128)} %bitcast.14, f32[]{:T(128)} %bitcast.13, f32[]{:T(128)} %bitcast.12, f32[]{:T(128)} %bitcast.11, f32[]{:T(128)} %bitcast.10, f32[]{:T(128)} %bitcast.9, f32[]{:T(128)} %bitcast.8, f32[]{:T(128)} %bitcast.7, f32[]{:T(128)} %bitcast.6, f32[]{:T(128)} %bitcast.5, ...), kind=kLoop, calls=%fused_computation.92 | loop fusion | flops 638976 | bytes 35132 | tf_op jit(solution)/shard_map/convert_element_type | solution.py:20
  179.5 10.2 %fusion.64 = bf16[128,128]{1,0:T(8,128)(2,1)} fusion(f32[]{:T(128)} %bitcast.30, f32[]{:T(128)} %bitcast.29, f32[]{:T(128)} %bitcast.28, f32[]{:T(128)} %bitcast.27, f32[]{:T(128)} %bitcast.26, f32[]{:T(128)} %bitcast.25, f32[]{:T(128)} %bitcast.24, f32[]{:T(128)} %bitcast.23, f32[]{:T(128)} %bitcast.22, f32[]{:T(128)} %bitcast.21, f32[]{:T(128)} %bitcast.20, ...), kind=kLoop, calls=%fused_computation.121 | loop fusion | flops 655360 | bytes 35132 | tf_op jit(solution)/shard_map/convert_element_type | solution.py:20
  189.7 10.2 %reduce-precision_convert_fusion.7 = bf16[128,128]{1,0:T(8,128)(2,1)} fusion(f32[]{:T(128)} %bitcast.30, f32[]{:T(128)} %bitcast.29, f32[]{:T(128)} %bitcast.28, f32[]{:T(128)} %bitcast.27, f32[]{:T(128)} %bitcast.26, f32[]{:T(128)} %bitcast.25, f32[]{:T(128)} %bitcast.24, f32[]{:T(128)} %bitcast.23, f32[]{:T(128)} %bitcast.22, f32[]{:T(128)} %bitcast.21, ...), kind=kLoop, calls=%fused_computation.90 | loop fusion | flops 638976 | bytes 35132 | tf_op jit(solution)/shard_map/convert_element_type | solution.py:20
  199.9 10.1 %fusion.65 = bf16[128,128]{1,0:T(8,128)(2,1)} fusion(f32[]{:T(128)} %bitcast.46, f32[]{:T(128)} %bitcast.45, f32[]{:T(128)} %bitcast.44, f32[]{:T(128)} %bitcast.43, f32[]{:T(128)} %bitcast.42, f32[]{:T(128)} %bitcast.41, f32[]{:T(128)} %bitcast.40, f32[]{:T(128)} %bitcast.39, f32[]{:T(128)} %bitcast.38, f32[]{:T(128)} %bitcast.37, f32[]{:T(128)} %bitcast.36, ...), kind=kLoop, calls=%fused_computation.122 | loop fusion | flops 655360 | bytes 35132 | tf_op jit(solution)/shard_map/convert_element_type | solution.py:20
  210.0 10.1 %reduce-precision_convert_fusion.6 = bf16[128,128]{1,0:T(8,128)(2,1)} fusion(f32[]{:T(128)} %bitcast.46, f32[]{:T(128)} %bitcast.45, f32[]{:T(128)} %bitcast.44, f32[]{:T(128)} %bitcast.43, f32[]{:T(128)} %bitcast.42, f32[]{:T(128)} %bitcast.41, f32[]{:T(128)} %bitcast.40, f32[]{:T(128)} %bitcast.39, f32[]{:T(128)} %bitcast.38, f32[]{:T(128)} %bitcast.37, ...), kind=kLoop, calls=%fused_computation.88 | loop fusion | flops 638976 | bytes 35132 | tf_op jit(solution)/shard_map/convert_element_type | solution.py:20
  220.1 10.0 %fusion.141 = bf16[64,128]{1,0:T(8,128)(2,1)} fusion(f32[]{:T(128)} %bitcast.14, f32[]{:T(128)} %bitcast.13, f32[]{:T(128)} %bitcast.12, f32[]{:T(128)} %bitcast.11, f32[]{:T(128)} %bitcast.10, f32[]{:T(128)} %bitcast.9, f32[]{:T(128)} %bitcast.8, f32[]{:T(128)} %bitcast.7, f32[]{:T(128)} %bitcast.6, f32[]{:T(128)} %bitcast.5, f32[]{:T(128)} %bitcast.4, ...), kind=kLoop, calls=%fused_computation.244 | loop fusion | flops 335872 | bytes 19900 | tf_op jit(solution)/shard_map/convert_element_type | solution.py:20
  230.1 10.0 %reduce-precision_convert_fusion.23 = bf16[64,128]{1,0:T(8,128)(2,1)} fusion(f32[]{:T(128)} %bitcast.14, f32[]{:T(128)} %bitcast.13, f32[]{:T(128)} %bitcast.12, f32[]{:T(128)} %bitcast.11, f32[]{:T(128)} %bitcast.10, f32[]{:T(128)} %bitcast.9, f32[]{:T(128)} %bitcast.8, f32[]{:T(128)} %bitcast.7, f32[]{:T(128)} %bitcast.6, f32[]{:T(128)} %bitcast.5, ...), kind=kLoop, calls=%fused_computation.243 | loop fusion | flops 327680 | bytes 19900 | tf_op jit(solution)/shard_map/convert_element_type | solution.py:20
  240.1 10.1 %fusion.142 = bf16[64,128]{1,0:T(8,128)(2,1)} fusion(f32[]{:T(128)} %bitcast.30, f32[]{:T(128)} %bitcast.29, f32[]{:T(128)} %bitcast.28, f32[]{:T(128)} %bitcast.27, f32[]{:T(128)} %bitcast.26, f32[]{:T(128)} %bitcast.25, f32[]{:T(128)} %bitcast.24, f32[]{:T(128)} %bitcast.23, f32[]{:T(128)} %bitcast.22, f32[]{:T(128)} %bitcast.21, f32[]{:T(128)} %bitcast.20, ...), kind=kLoop, calls=%fused_computation.245 | loop fusion | flops 335872 | bytes 19900 | tf_op jit(solution)/shard_map/convert_element_type | solution.py:20
  250.3 10.2 %reduce-precision_convert_fusion.22 = bf16[64,128]{1,0:T(8,128)(2,1)} fusion(f32[]{:T(128)} %bitcast.30, f32[]{:T(128)} %bitcast.29, f32[]{:T(128)} %bitcast.28, f32[]{:T(128)} %bitcast.27, f32[]{:T(128)} %bitcast.26, f32[]{:T(128)} %bitcast.25, f32[]{:T(128)} %bitcast.24, f32[]{:T(128)} %bitcast.23, f32[]{:T(128)} %bitcast.22, f32[]{:T(128)} %bitcast.21, ...), kind=kLoop, calls=%fused_computation.241 | loop fusion | flops 327680 | bytes 19900 | tf_op jit(solution)/shard_map/convert_element_type | solution.py:20
  260.4 10.0 %fusion.143 = bf16[64,128]{1,0:T(8,128)(2,1)} fusion(f32[]{:T(128)} %bitcast.46, f32[]{:T(128)} %bitcast.45, f32[]{:T(128)} %bitcast.44, f32[]{:T(128)} %bitcast.43, f32[]{:T(128)} %bitcast.42, f32[]{:T(128)} %bitcast.41, f32[]{:T(128)} %bitcast.40, f32[]{:T(128)} %bitcast.39, f32[]{:T(128)} %bitcast.38, f32[]{:T(128)} %bitcast.37, f32[]{:T(128)} %bitcast.36, ...), kind=kLoop, calls=%fused_computation.246 | loop fusion | flops 335872 | bytes 19900 | tf_op jit(solution)/shard_map/convert_element_type | solution.py:20
  270.5 10.0 %reduce-precision_convert_fusion.21 = bf16[64,128]{1,0:T(8,128)(2,1)} fusion(f32[]{:T(128)} %bitcast.46, f32[]{:T(128)} %bitcast.45, f32[]{:T(128)} %bitcast.44, f32[]{:T(128)} %bitcast.43, f32[]{:T(128)} %bitcast.42, f32[]{:T(128)} %bitcast.41, f32[]{:T(128)} %bitcast.40, f32[]{:T(128)} %bitcast.39, f32[]{:T(128)} %bitcast.38, f32[]{:T(128)} %bitcast.37, ...), kind=kLoop, calls=%fused_computation.239 | loop fusion | flops 327680 | bytes 19900 | tf_op jit(solution)/shard_map/convert_element_type | solution.py:20
  280.5 10.0 %fusion.144 = bf16[64,128]{1,0:T(8,128)(2,1)} fusion(f32[]{:T(128)} %bitcast.14, f32[]{:T(128)} %bitcast.13, f32[]{:T(128)} %bitcast.12, f32[]{:T(128)} %bitcast.11, f32[]{:T(128)} %bitcast.10, f32[]{:T(128)} %bitcast.9, f32[]{:T(128)} %bitcast.8, f32[]{:T(128)} %bitcast.7, f32[]{:T(128)} %bitcast.6, f32[]{:T(128)} %bitcast.5, f32[]{:T(128)} %bitcast.4, ...), kind=kLoop, calls=%fused_computation.247 | loop fusion | flops 335872 | bytes 19900 | tf_op jit(solution)/shard_map/convert_element_type | solution.py:20
  290.5 10.0 %reduce-precision_convert_fusion.20 = bf16[64,128]{1,0:T(8,128)(2,1)} fusion(f32[]{:T(128)} %bitcast.14, f32[]{:T(128)} %bitcast.13, f32[]{:T(128)} %bitcast.12, f32[]{:T(128)} %bitcast.11, f32[]{:T(128)} %bitcast.10, f32[]{:T(128)} %bitcast.9, f32[]{:T(128)} %bitcast.8, f32[]{:T(128)} %bitcast.7, f32[]{:T(128)} %bitcast.6, f32[]{:T(128)} %bitcast.5, ...), kind=kLoop, calls=%fused_computation.237 | loop fusion | flops 327680 | bytes 19900 | tf_op jit(solution)/shard_map/convert_element_type | solution.py:20
  300.5 10.1 %fusion.145 = bf16[64,128]{1,0:T(8,128)(2,1)} fusion(f32[]{:T(128)} %bitcast.30, f32[]{:T(128)} %bitcast.29, f32[]{:T(128)} %bitcast.28, f32[]{:T(128)} %bitcast.27, f32[]{:T(128)} %bitcast.26, f32[]{:T(128)} %bitcast.25, f32[]{:T(128)} %bitcast.24, f32[]{:T(128)} %bitcast.23, f32[]{:T(128)} %bitcast.22, f32[]{:T(128)} %bitcast.21, f32[]{:T(128)} %bitcast.20, ...), kind=kLoop, calls=%fused_computation.248 | loop fusion | flops 335872 | bytes 19900 | tf_op jit(solution)/shard_map/convert_element_type | solution.py:20
  310.7 10.1 %reduce-precision_convert_fusion.19 = bf16[64,128]{1,0:T(8,128)(2,1)} fusion(f32[]{:T(128)} %bitcast.30, f32[]{:T(128)} %bitcast.29, f32[]{:T(128)} %bitcast.28, f32[]{:T(128)} %bitcast.27, f32[]{:T(128)} %bitcast.26, f32[]{:T(128)} %bitcast.25, f32[]{:T(128)} %bitcast.24, f32[]{:T(128)} %bitcast.23, f32[]{:T(128)} %bitcast.22, f32[]{:T(128)} %bitcast.21, ...), kind=kLoop, calls=%fused_computation.235 | loop fusion | flops 327680 | bytes 19900 | tf_op jit(solution)/shard_map/convert_element_type | solution.py:20
  320.8 10.0 %fusion.146 = bf16[64,128]{1,0:T(8,128)(2,1)} fusion(f32[]{:T(128)} %bitcast.46, f32[]{:T(128)} %bitcast.45, f32[]{:T(128)} %bitcast.44, f32[]{:T(128)} %bitcast.43, f32[]{:T(128)} %bitcast.42, f32[]{:T(128)} %bitcast.41, f32[]{:T(128)} %bitcast.40, f32[]{:T(128)} %bitcast.39, f32[]{:T(128)} %bitcast.38, f32[]{:T(128)} %bitcast.37, f32[]{:T(128)} %bitcast.36, ...), kind=kLoop, calls=%fused_computation.249 | loop fusion | flops 335872 | bytes 19900 | tf_op jit(solution)/shard_map/convert_element_type | solution.py:20
  330.9 10.0 %reduce-precision_convert_fusion.18 = bf16[64,128]{1,0:T(8,128)(2,1)} fusion(f32[]{:T(128)} %bitcast.46, f32[]{:T(128)} %bitcast.45, f32[]{:T(128)} %bitcast.44, f32[]{:T(128)} %bitcast.43, f32[]{:T(128)} %bitcast.42, f32[]{:T(128)} %bitcast.41, f32[]{:T(128)} %bitcast.40, f32[]{:T(128)} %bitcast.39, f32[]{:T(128)} %bitcast.38, f32[]{:T(128)} %bitcast.37, ...), kind=kLoop, calls=%fused_computation.233 | loop fusion | flops 327680 | bytes 19900 | tf_op jit(solution)/shard_map/convert_element_type | solution.py:20
  344.2 0.7 copy-done.27
  345.0 0.7 copy-done.29
  345.8 0.7 copy-done.21
  346.5 0.7 copy-done.25
  347.3 0.7 copy-done.19
  348.1 0.7 copy-done.17
  348.9 0.7 copy-done.15
  349.6 0.7 copy-done.13
  350.4 0.7 copy-done.11
  354.9 0.7 copy-done.23
  356.7 0.8 copy-done.1
  357.6 24.9 %scatter.1 = f32[8,32,8,64]{3,2,1,0:T(8,128)} custom-call(s32[40,2]{1,0:T(8,128)} %copy.7.wav, s32[32,2]{1,0:T(8,128)} %copy.8.pairs, f32[15]{0:T(128)} %even.1, f32[15]{0:T(128)} %odd.1, f32[15]{0:T(128)} %low.1, f32[42,16,128]{2,1,0:T(8,128)} %copy-done.4, f32[64,16,128]{2,1,0:T(8,128)} %centre.1, f32[42,16,128]{2,1,0:T(8,128)} %collective-permute-done.1.after, ...), custom_call_target="tpu_custom_call" | custom-call | tf_op jit(solution)/shard_map/scatter/pallas_call | solution.py:264
  (119 shorter events, 10.5 us)
Async XLA Ops:
  1.2 355.4 %collective-permute-start = (f32[42,16,128]{2,1,0:T(8,128)S(1)}, f32[42,16,128]{2,1,0:T(8,128)S(1)}, u32[]{:S(2)}, u32[]{:S(2)}) collective-permute-start(f32[42,16,128]{2,1,0:T(8,128)S(1)} %get-tuple-element.6), channel_id=1, source_target_pairs={{0,4},{4,8},{8,12},{1,5},{5,9},{9,13},{2,6},{6,10},{10,14},{3,7},{... | collective-permute-start | bytes 1032200 | tf_op jit(solution)/shard_map/ppermute | solution.py:257
  6.2 1.3 copy-start.8
  6.2 350.4 %collective-permute-start.1 = (f32[42,16,128]{2,1,0:T(8,128)S(1)}, f32[42,16,128]{2,1,0:T(8,128)}, u32[]{:S(2)}, u32[]{:S(2)}) collective-permute-start(f32[42,16,128]{2,1,0:T(8,128)S(1)} %get-tuple-element.5), channel_id=1, source_target_pairs={{4,0},{8,4},{12,8},{5,1},{9,5},{13,9},{6,2},{10,6},{14,10},{7,3},{... | collective-permute-start | bytes 1032200 | tf_op jit(solution)/shard_map/ppermute | solution.py:258
  28.3 10.1 %copy-start.9 = (f32[15]{0:T(128)S(1)}, f32[15]{0:T(128)}, u32[]{:S(2)}) copy-start(f32[15]{0:T(128)} %odd.1) | copy-start | bytes 184
  59.4 10.2 %copy-start.10 = (f32[15]{0:T(128)S(1)}, f32[15]{0:T(128)}, u32[]{:S(2)}) copy-start(f32[15]{0:T(128)} %low.1) | copy-start | bytes 184
  341.4 0.7 copy-start.44
  342.1 0.7 copy-start.43
  343.5 0.7 copy-start.41
  343.5 0.7 copy-start.42
  344.2 0.8 copy-start.27
  344.2 0.8 copy-start.28
  345.0 0.8 copy-start.29
  345.0 0.8 copy-start.30
  345.8 0.8 copy-start.21
  345.8 0.8 copy-start.22
  346.5 0.8 copy-start.25
  346.5 0.8 copy-start.26
  347.3 0.8 copy-start.19
  347.3 0.8 copy-start.20
  348.1 0.8 copy-start.17
  348.1 0.8 copy-start.18
  348.8 0.8 copy-start.15
  348.9 0.8 copy-start.16
  349.6 0.8 copy-start.13
  349.6 0.8 copy-start.14
  350.4 0.8 copy-start.11
  350.4 0.8 copy-start.12
  351.2 0.7 copy-start.35
  351.2 0.7 copy-start.36
  351.9 4.7 %copy-start.2 = (bf16[6,128,384]{2,1,0:T(8,128)(2,1)}, bf16[6,128,384]{2,1,0:T(8,128)(2,1)S(1)}, u32[]{:S(2)}) copy-start(bf16[6,128,384]{2,1,0:T(8,128)(2,1)S(1)} %fusion.53.y1) | copy-start | bytes 1769476
  351.9 0.7 copy-start.33
  351.9 0.8 copy-start.34
  352.7 0.7 copy-start.31
  352.7 0.7 copy-start.32
  353.4 0.7 copy-start.37
  353.4 0.7 copy-start.38
  354.2 0.7 copy-start.39
  354.2 0.7 copy-start.40
  354.9 0.8 copy-start.23
  354.9 0.8 copy-start.24
  354.9 1.7 copy-start.3
  355.7 0.8 copy-start.5
  355.7 0.8 copy-start.6
  355.7 0.8 copy-start.7
  355.7 0.9 copy-start
  356.6 0.9 copy-start.1
  356.6 1.0 copy-start.4
where the time goes:
time: 389 us; the launch traced here: 382 us
  other arithmetic  332 us (85%)
  Pallas kernels  24.9 us (6%)
  local copies, waits for them, and re-layouts  18.9 us (5%)
  starting transfers between devices  6.27 us (2%)
    convert_element_type x33, other arithmetic, split_outside(): return (hi.astype(BF), (t - hi).astype(BF))  331 us
    pallas_call x1, Pallas kernels, shards(): pl.pallas_call(functools.partial(kernel, rows), out_shape=jax.ShapeDtypeS...  24.9 us
    unnamed x92, local copies, waits for them, and re-layouts  15.6 us
  transfers between devices with their start and end apart: 2, of which 0 were waited for; matrix products, arithmetic and copies ran while one was open for 88% of the time, Pallas kernels for 0%

commit v1 on v0

--- a/solution.py
+++ b/solution.py
@@ -12,72 +12,149 @@
 REACH2 = 28
 HALO = REACH1 + REACH2
 GROUP = 8
+CHUNKS = 3
 BF = jnp.bfloat16
-
-
-def split_outside(t):
-    hi = lax.reduce_precision(t, 8, 7)
-    return hi.astype(BF), (t - hi).astype(BF)
-
-
-def band(diff, taps, dilation):
-    count = taps.shape[0]
-    total = jnp.zeros(diff.shape, jnp.float32)
-    for t in range(count):
-        total = jnp.where(diff == (t - count // 2) * dilation, taps[t], total)
-    return total
-
-
-def tables(filters, ny, nz):
-    def zdiff(n_out, stride):
-        i = lax.broadcasted_iota(jnp.int32, (nz, n_out), 0)
-        j = lax.broadcasted_iota(jnp.int32, (nz, n_out), 1)
-        return i - j * stride
-
-    def ytable(taps, d, stride):
-        n_out = ny // stride
-        r = lax.broadcasted_iota(jnp.int32, (GROUP * n_out, GROUP * ny), 0)
-        c = lax.broadcasted_iota(jnp.int32, (GROUP * n_out, GROUP * ny), 1)
-        t = band(c % ny - (r % n_out) * stride, taps, d)
-        hi, lo = split_outside(jnp.where(r // n_out == c // ny, t, 0.0))
-        return jnp.concatenate([hi, hi, lo], axis=1)
-
-    z1, y1, z2, y2 = [], [], [], []
-    for level in (0, 1):
-        for taps in filters:
-            hi, lo = split_outside(band(zdiff(nz, 1), taps, 1 << level))
-            z1.append(
-                jnp.concatenate(
-                    [
-                        jnp.concatenate([hi, lo], axis=1),
-                        jnp.concatenate([hi, jnp.zeros_like(lo)], axis=1),
-                    ],
-                    axis=0,
-                )
-            )
-            y1.append(ytable(taps, 1 << level, 1))
-    for level in (1, 2):
-        parts = [split_outside(band(zdiff(nz // 2, 2), taps, 1 << level)) for taps in filters]
-        zero = jnp.zeros((nz, nz // 2), BF)
-        none = (zero, zero)
-        for left, right in ((parts[2], none), (none, parts[2]), (parts[0], parts[1])):
-            z2.append(
-                jnp.concatenate(
-                    [
-                        jnp.concatenate([left[0], right[0], left[1], right[1]], axis=1),
-                        jnp.concatenate([left[0], right[0], zero, zero], axis=1),
-                    ],
-                    axis=0,
-                )
-            )
-        for taps in filters:
-            y2.append(ytable(taps, 1 << level, 2))
-    return jnp.stack(z1), jnp.stack(y1), jnp.stack(z2), jnp.stack(y2)
 
 
 def halves(v):
     hi = v.astype(BF)
     return hi, (v - hi.astype(jnp.float32)).astype(BF)
+
+
+def band(diff, tap_sets, dilation, extent):
+    count = tap_sets[0].shape[0]
+    totals = [jnp.zeros(diff.shape, jnp.float32) for _ in tap_sets]
+    for t in range(count):
+        offset = (t - count // 2) * dilation
+        if abs(offset) < extent:
+            hit = diff == offset
+            totals = [jnp.where(hit, s[t], v) for s, v in zip(tap_sets, totals)]
+    return totals
+
+
+def build_tables(filters, ny, nz, z1, y1, z2, y2):
+    even, odd, low = filters
+    blk = 32
+
+    def iotas(r0, shape):
+        r = lax.broadcasted_iota(jnp.int32, shape, 0) + r0
+        return r, lax.broadcasted_iota(jnp.int32, shape, 1)
+
+    def put_z(ref, n, r0, value):
+        hi, lo = halves(value)
+        ref[n, pl.ds(r0, blk), pl.ds(0, nz)] = hi
+        ref[n, pl.ds(r0, blk), pl.ds(nz, nz)] = lo
+        ref[n, pl.ds(nz + r0, blk), pl.ds(0, nz)] = hi
+        ref[n, pl.ds(nz + r0, blk), pl.ds(nz, nz)] = jnp.zeros_like(lo)
+
+    def put_y(ref, n, r0, value):
+        hi, lo = halves(value)
+        width = GROUP * ny
+        ref[n, pl.ds(r0, blk), pl.ds(0, width)] = hi
+        ref[n, pl.ds(r0, blk), pl.ds(width, width)] = hi
+        ref[n, pl.ds(r0, blk), pl.ds(2 * width, width)] = lo
+
+    for level in (0, 1):
+        for r0 in range(0, nz, blk):
+            i, j = iotas(r0, (blk, nz))
+            for n, v in enumerate(band(i - j, filters, 1 << level, nz)):
+                put_z(z1, level * 3 + n, r0, v)
+    for stride, ref, levels in ((1, y1, (0, 1)), (2, y2, (1, 2))):
+        n_out = ny // stride
+        for r0 in range(0, GROUP * n_out, blk):
+            r, c = iotas(r0, (blk, GROUP * ny))
+            diff = jnp.where(r // n_out == c // ny, c % ny - (r % n_out) * stride, 4 * ny)
+            for at, level in enumerate(levels):
+                for n, v in enumerate(band(diff, filters, 1 << level, ny)):
+                    put_y(ref, at * 3 + n, r0, v)
+    half = nz // 2
+    for at, level in enumerate((1, 2)):
+        for r0 in range(0, nz, blk):
+            i, j = iotas(r0, (blk, nz))
+            left = j < half
+            diff = i - 2 * jnp.where(left, j, j - half)
+            e, o, l = band(diff, filters, 1 << level, nz)
+            put_z(z2, at * 3, r0, jnp.where(left, l, 0.0))
+            put_z(z2, at * 3 + 1, r0, jnp.where(left, 0.0, l))
+            put_z(z2, at * 3 + 2, r0, jnp.where(left, e, o))
+
+
+def exchange(even, odd, low, density, before, after, z1, y1, z2, y2, zsend, zrecv, psend, precv):
+    rows, ny, nz = density.shape
+    chunk = HALO // 2 // CHUNKS
+    count = lax.axis_size("space")
+    space = lax.axis_index("space")
+    wave = lax.axis_index("wave")
+    core = lax.rem(wave, 2)
+    partner = wave + 1 - 2 * core
+    above = space < count - 1
+    below = space > 0
+    mesh_ids = pl.DeviceIdType.MESH
+    barrier = pltpu.get_barrier_semaphore()
+
+    @pl.when(above)
+    def _():
+        pl.semaphore_signal(barrier, 1, device_id={"space": space + 1}, device_id_type=mesh_ids)
+
+    @pl.when(below)
+    def _():
+        pl.semaphore_signal(barrier, 1, device_id={"space": space - 1}, device_id_type=mesh_ids)
+
+    pl.semaphore_signal(barrier, 1, device_id={"wave": partner}, device_id_type=mesh_ids)
+    peers = 1 + above.astype(jnp.int32) + below.astype(jnp.int32)
+    pl.semaphore_wait(barrier, peers)
+
+    landing = (before, after)
+    sends = (above, below)
+    arrives = (below, above)
+
+    def zcopy(way, q):
+        r = core * (HALO // 2) + q * chunk
+        return pltpu.make_async_remote_copy(
+            src_ref=density.at[pl.ds(r + (rows - HALO if way == 0 else 0), chunk)],
+            dst_ref=landing[way].at[pl.ds(r, chunk)],
+            send_sem=zsend.at[way, q],
+            recv_sem=zrecv.at[way, q],
+            device_id={"space": space + 1 if way == 0 else space - 1},
+            device_id_type=mesh_ids,
+        )
+
+    def pcopy(way, q, first):
+        part = landing[way].at[pl.ds(first * (HALO // 2) + q * chunk, chunk)]
+        return pltpu.make_async_remote_copy(
+            src_ref=part,
+            dst_ref=part,
+            send_sem=psend.at[way, q],
+            recv_sem=precv.at[way, q],
+            device_id={"wave": partner},
+            device_id_type=mesh_ids,
+        )
+
+    every = [(way, q) for q in range(CHUNKS) for way in range(2)]
+    for way, q in every:
+
+        @pl.when(sends[way])
+        def _():
+            zcopy(way, q).start()
+
+    build_tables((even, odd, low), ny, nz, z1, y1, z2, y2)
+    for way, q in every:
+
+        @pl.when(arrives[way])
+        def _():
+            zcopy(way, q).wait_recv()
+            pcopy(way, q, core).start()
+
+    for way, q in every:
+
+        @pl.when(sends[way])
+        def _():
+            zcopy(way, q).wait_send()
+
+        @pl.when(arrives[way])
+        def _():
+            pcopy(way, q, core).wait_send()
+            pcopy(way, q, 1 - core).wait_recv()
 
 
 def stacked(v):
@@ -135,16 +212,35 @@
     per_dev = out.shape[0]
     taps_half = even.shape[0] // 2
     fields = rows + 2 * REACH2
-    copies = [
-        pltpu.make_async_copy(before, ext.at[pl.ds(0, HALO)], sems.at[0]),
-        pltpu.make_async_copy(centre, ext.at[pl.ds(HALO, rows)], sems.at[1]),
-        pltpu.make_async_copy(after, ext.at[pl.ds(HALO + rows, HALO)], sems.at[2]),
-    ]
-    for copy in copies:
-        copy.start()
-    for copy in copies:
-        copy.wait()
     space = lax.axis_index("space")
+    last = lax.axis_size("space") - 1
+    inner = pltpu.make_async_copy(centre, ext.at[pl.ds(HALO, rows)], sems.at[1])
+    inner.start()
+    edges = (
+        (space > 0, pltpu.make_async_copy(before, ext.at[pl.ds(0, HALO)], sems.at[0]), 0),
+        (
+            space < last,
+            pltpu.make_async_copy(after, ext.at[pl.ds(HALO + rows, HALO)], sems.at[2]),
+            HALO + rows,
+        ),
+    )
+    for there, copy, at in edges:
+
+        @pl.when(there)
+        def _():
+            copy.start()
+
+        @pl.when(jnp.logical_not(there))
+        def _():
+            ext[pl.ds(at, HALO)] = jnp.zeros((HALO, ny, nz), jnp.float32)
+
+    for there, copy, _ in edges:
+
+        @pl.when(there)
+        def _():
+            copy.wait()
+
+    inner.wait()
     start = lax.axis_index("wave") * per_dev
 
     def first_steps(f, orient, unroll):
@@ -195,7 +291,7 @@
         def _():
             firsts[f, pl.ds(0, REACH2)] = jnp.zeros((REACH2, ny, nz), jnp.float32)
 
-        @pl.when(space == lax.axis_size("space") - 1)
+        @pl.when(space == last)
         def _():
             firsts[f, pl.ds(REACH2 + rows, REACH2)] = jnp.zeros((REACH2, ny, nz), jnp.float32)
 
@@ -251,16 +347,29 @@
 
 def shards(density, even_taps, odd_taps, low_taps, wavelets, pairs):
     rows, ny, nz = density.shape
-    count = lax.axis_size("space")
-    up = [(i, i + 1) for i in range(count - 1)]
-    down = [(j, i) for i, j in up]
-    before = lax.ppermute(density[rows - HALO :], "space", up)
-    after = lax.ppermute(density[:HALO], "space", down)
-    z1, y1, z2, y2 = tables((even_taps, odd_taps, low_taps), ny, nz)
     per_dev = pairs.shape[0] // lax.axis_size("wave")
     smem = pl.BlockSpec(memory_space=pltpu.SMEM)
     vmem = pl.BlockSpec(memory_space=pltpu.VMEM)
     anyw = pl.BlockSpec(memory_space=pl.ANY)
+    halo = jax.ShapeDtypeStruct((HALO, ny, nz), jnp.float32)
+    before, after, z1, y1, z2, y2 = pl.pallas_call(
+        exchange,
+        out_shape=(
+            halo,
+            halo,
+            jax.ShapeDtypeStruct((6, 2 * nz, 2 * nz), BF),
+            jax.ShapeDtypeStruct((6, GROUP * ny, 3 * GROUP * ny), BF),
+            jax.ShapeDtypeStruct((6, 2 * nz, 2 * nz), BF),
+            jax.ShapeDtypeStruct((6, GROUP * ny // 2, 3 * GROUP * ny), BF),
+        ),
+        in_specs=[smem] * 3 + [anyw],
+        out_specs=[anyw] * 2 + [vmem] * 4,
+        scratch_shapes=[pltpu.SemaphoreType.DMA((2, CHUNKS))] * 4,
+        compiler_params=pltpu.CompilerParams(
+            collective_id=0, has_side_effects=True, vmem_limit_bytes=16 << 20
+        ),
+        name="exchange",
+    )(even_taps, odd_taps, low_taps, density)
     return pl.pallas_call(
         functools.partial(kernel, rows),
         out_shape=jax.ShapeDtypeStruct((per_dev, rows // 2, ny // 2, nz // 2), jnp.float32),
@@ -271,6 +380,7 @@
             pltpu.VMEM((NFIRST, rows + 2 * REACH2, ny, nz), jnp.float32),
             pltpu.SemaphoreType.DMA((3,)),
         ],
+        compiler_params=pltpu.CompilerParams(vmem_limit_bytes=24 << 20),
         name="scatter",
     )(wavelets, pairs, even_taps, odd_taps, low_taps, before, density, after, z1, y1, z2, y2)
 

time: 389 us -> 35.2 us (0.09); the launches traced: 382 us -> 35.2 us
  other arithmetic: 332 us -> 0 us
  local copies, waits for them, and re-layouts: 18.9 us -> 2.5 us
  Pallas kernels: 24.9 us -> 32.7 us
  starting transfers between devices: 6.27 us -> 0 us
    convert_element_type x33 -> x0, other arithmetic: 331 us -> none  [split_outside(): return (hi.astype(BF), (t - hi).astype(BF))]
    unnamed x92 -> x14, local copies, waits for them, and re-layouts: 15.6 us -> 2.5 us
    pallas_call x0 -> x1, Pallas kernels: none -> 10.4 us  [shards(): pl.pallas_call(exchange, out_shape=(halo, halo, jax.ShapeDtypeStruct((6,...]
    ppermute x2 -> x0, starting transfers between devices: 6.27 us -> none  [the longest x1 4.98 us: shards(): before = lax.ppermute(density[rows - HALO:], 'space', up)]
  transfers between devices with their start and end apart: 2 -> 0, of which waited for: 0 -> 0; matrix products, arithmetic and copies ran while one was open for 88% -> 0% of each run, Pallas kernels for 0% -> 0%
where the time goes in v1:
time: 35.2 us
  Pallas kernels  32.7 us (93%)
  local copies, waits for them, and re-layouts  2.5 us (7%)
    pallas_call x1, Pallas kernels, shards(): pl.pallas_call(functools.partial(kernel, rows), out_shape=jax.ShapeDtypeS...  22.2 us
    pallas_call x1, Pallas kernels, shards(): pl.pallas_call(exchange, out_shape=(halo, halo, jax.ShapeDtypeStruct((6,...  10.4 us
    unnamed x14, local copies, waits for them, and re-layouts  2.5 us

profile of v1, /device:TPU:0, one launch (start us, length us, event | category | flops | bytes accessed | tf_op | source)
XLA Modules:
  0.0 35.2 jit_solution(4410871181725422001)
XLA Ops:
  0.0 0.0 copy-start.5
  0.0 0.8 %copy.8.pairs = s32[32,2]{1,0:T(8,128)S(1)} copy(s32[32,2]{0,1:T(2,128)} %param.11) | data formatting | bytes 512 | tf_op args[5]
  0.8 0.0 copy-done.5
  0.8 0.0 copy-start.2
  0.8 0.0 copy-start.3
  0.8 0.0 copy-start.4
  0.8 0.1 copy.7.wav
  0.9 0.5 %copy-done.2 = f32[15]{0:T(128)S(1)} copy-done((f32[15]{0:T(128)S(1)}, f32[15]{0:T(128)}, u32[]{:S(2)}) %copy-start.2) | copy-done | bytes 84
  1.4 0.0 copy-done.3
  1.5 0.0 copy-done.4
  1.5 0.0 copy-start
  1.5 1.0 %copy-done = f32[64,16,128]{2,1,0:T(8,128)S(1)} copy-done((f32[64,16,128]{2,1,0:T(8,128)S(1)}, f32[64,16,128]{2,1,0:T(8,128)}, u32[]{:S(2)}) %copy-start) | copy-done | bytes 524312
  2.5 0.0 copy-start.1
  2.5 10.4 %exchange.1 = (f32[42,16,128]{2,1,0:T(8,128)S(1)}, f32[42,16,128]{2,1,0:T(8,128)S(1)}, bf16[6,256,256]{2,1,0:T(8,128)(2,1)S(1)}, bf16[6,128,384]{2,1,0:T(8,128)(...) custom-call(f32[15]{0:T(128)S(1)} %copy-done.2, f32[15]{0:T(128)S(1)} %copy-done.3, ...), custom_call_target="tpu_custom_call" | custom-call | tf_op jit(solution)/shard_map/exchange/pallas_call | solution.py:355
  12.9 0.0 copy-done.1
  12.9 22.2 %scatter.1 = f32[8,32,8,64]{3,2,1,0:T(8,128)} custom-call(s32[40,2]{1,0:T(8,128)S(1)} %copy.7.wav, s32[32,2]{1,0:T(8,128)S(1)} %copy.8.pairs, f32[15]{0:T(128)S(1)} %copy-done.2, f32[15]{0:T(128)S(1)} %copy-done.3, f32[15]{0:T(128)S(1)} %copy-done.4, f32[42,16,128]{2,1,0:T(8,128)S(1)} %get-tuple-element.11.before, f32[64,16,128]{2,1,0:T(8,128)S(1)} %copy-done.1, ...), custom_call_target="tpu_custom_call" | custom-call | tf_op jit(solution)/shard_map/scatter/pallas_call | solution.py:373
Async XLA Ops:
  0.0 0.8 %copy-start.5 = (s32[40,2]{0,1:T(2,128)S(1)}, s32[40,2]{0,1:T(2,128)}, u32[]{:S(2)}) copy-start(s32[40,2]{0,1:T(2,128)} %param.10) | copy-start | bytes 964
  0.8 0.7 %copy-start.2 = (f32[15]{0:T(128)S(1)}, f32[15]{0:T(128)}, u32[]{:S(2)}) copy-start(f32[15]{0:T(128)} %even.3) | copy-start | bytes 184
  0.8 0.7 %copy-start.3 = (f32[15]{0:T(128)S(1)}, f32[15]{0:T(128)}, u32[]{:S(2)}) copy-start(f32[15]{0:T(128)} %odd.3) | copy-start | bytes 184
  0.8 0.7 %copy-start.4 = (f32[15]{0:T(128)S(1)}, f32[15]{0:T(128)}, u32[]{:S(2)}) copy-start(f32[15]{0:T(128)} %low.3) | copy-start | bytes 184
  1.5 1.0 %copy-start = (f32[64,16,128]{2,1,0:T(8,128)S(1)}, f32[64,16,128]{2,1,0:T(8,128)}, u32[]{:S(2)}) copy-start(f32[64,16,128]{2,1,0:T(8,128)} %centre.1) | copy-start | bytes 1572868
  2.5 10.4 %copy-start.1 = (f32[64,16,128]{2,1,0:T(8,128)S(1)}, f32[64,16,128]{2,1,0:T(8,128)}, u32[]{:S(2)}) copy-start(f32[64,16,128]{2,1,0:T(8,128)} %centre.1) | copy-start | bytes 1572868
